TPU v7x, 32 devices: a whole 2x2x4 slice. The times are simulated.
32 devices in a mesh: bx: 4 (over x, core), by: 4 (over z), bz: 2 (over y).
Axes of the slice: x: 2, y: 2, z: 4, core: 2. Of those that a mesh axis runs over, the one named last changes fastest.
Arguments:
- density: float32 [32, 512, 512], P('bz', 'bx', 'by'), may hold values from 0 to 1
- colors: float32 [3, 128], replicated, may hold values from 0 to 1
- extinction: float32 [128], replicated, may hold values from 0.001 to 0.06
- march_steps: int32 [4, 4, 2], P('bx', 'by'), may hold values from 1 to 16
- depth_rank: int32 [4, 4, 2], P('bx'), may hold values from 0 to 1, as said below
Outputs:
- image: float32 [5, 512, 512], P(None, ('bx', 'by', 'bz'))
Inputs may be any that keep to these rules, and one draw needn't show every extreme that they name: All columns share one view: either depth_rank[i, j, k] = k for every brick, or depth_rank[i, j, k] = 1 - k for every brick.
All inputs are finite; a program needn't handle non-finite values.
Results may differ from a plain program's by a relative error of at most 0.0017.
Values sent between devices are 32-bit elements; how exact they have to be, the bound alone decides.
A program may use at most 64 MiB of HBM per device.

v0:
```python
import jax
import jax.numpy as jnp
from jax import lax
from jax.sharding import PartitionSpec as P


def march(slab, count, rank, table, total, backward):
    pixels = slab.shape[1] * slab.shape[2]
    points = table.shape[1]
    cells = slab.shape[0]
    nodes = jnp.arange(points, dtype=jnp.int32)[:, None]
    upper = table.astype(jnp.bfloat16)
    lower = (table - upper.astype(table.dtype)).astype(jnp.bfloat16)
    halves = jnp.concatenate([upper, lower], 0)
    width = table.shape[0]

    def fetch(index):
        onehot = (nodes == index).astype(jnp.bfloat16)
        joined = jnp.dot(halves, onehot, preferred_element_type=jnp.float32)
        return joined[:width] + joined[width:]

    def step(cell, carry):
        color, depth, trans = carry
        inner = jnp.where(backward, cells - 1 - cell, cell).astype(jnp.int32)
        plane = lax.dynamic_index_in_dim(slab, inner, 0, keepdims=False).reshape(1, pixels)
        coord = plane * (points - 1)
        index = jnp.clip(jnp.floor(coord).astype(jnp.int32), 0, points - 2)
        frac = coord - index.astype(coord.dtype)
        values = fetch(index) * (1.0 - frac) + fetch(index + 1) * frac
        keep = jnp.exp(-values[3])
        weight = trans * (1.0 - keep)
        zpos = ((rank * cells + cell).astype(slab.dtype) + 0.5) / total
        return (color + weight[None] * values[:3], depth + weight * zpos, trans * keep)

    start = (
        jnp.zeros((3, pixels), slab.dtype),
        jnp.zeros((pixels,), slab.dtype),
        jnp.ones((pixels,), slab.dtype),
    )
    color, depth, trans = lax.fori_loop(0, count, step, start)
    return jnp.concatenate([color, depth[None], trans[None]], 0)


def composite(parts, ranks):
    layers = parts.shape[0]
    order = jnp.arange(layers, dtype=jnp.int32)
    pick = (ranks[:, None] == order[None, :]).astype(parts.dtype)
    ordered = jnp.einsum("kq,kcm->qcm", pick, parts, precision=lax.Precision.HIGHEST)
    color = jnp.zeros(ordered.shape[2:], parts.dtype)[None] * jnp.zeros((3, 1), parts.dtype)
    depth = jnp.zeros(ordered.shape[2:], parts.dtype)
    trans = jnp.ones(ordered.shape[2:], parts.dtype)
    for level in range(layers):
        color = color + trans[None] * ordered[level, :3]
        depth = depth + trans * ordered[level, 3]
        trans = trans * ordered[level, 4]
    return jnp.concatenate([color, depth[None], trans[None]], 0)


def deliver_rows(merged):
    return lax.all_to_all(merged, "by", split_axis=1, concat_axis=3, tiled=True)


def shards(density, colors, extinction, march_steps, depth_rank):
    n_by = lax.axis_size("by")
    n_bz = lax.axis_size("bz")
    depth_cells, tile_x, tile_y = density.shape
    rows = tile_x // (n_by * n_bz)
    total = depth_cells * n_bz
    table = jnp.concatenate([colors, extinction[None]], 0)
    column_steps = march_steps[0, 0]
    column_ranks = lax.dynamic_index_in_dim(depth_rank[0], lax.axis_index("by"), 0, keepdims=False)
    backward = depth_rank[0, 0, 0] != 0
    slab = density.reshape(depth_cells, n_by, n_bz, rows, tile_y)
    column = lax.all_to_all(slab, "bz", split_axis=2, concat_axis=0, tiled=True)
    column = column.reshape(n_bz, depth_cells, n_by * rows, tile_y)
    parts = jnp.stack(
        [
            march(column[layer], column_steps[layer], column_ranks[layer], table, total, backward)
            for layer in range(n_bz)
        ],
        0,
    )
    merged = composite(parts, column_ranks).reshape(5, n_by, rows, tile_y)
    result = deliver_rows(merged).reshape(5, rows, n_by * tile_y)
    return jnp.concatenate([result[:4], 1.0 - result[4:5]], 0)


def solution(mesh):
    return jax.shard_map(
        shards,
        mesh=mesh,
        in_specs=(P("bz", "bx", "by"), P(), P(), P("bx", "by", None), P("bx", None, None)),
        out_specs=P(None, ("bx", "by", "bz"), None),
        check_vma=False,
    )
```

profile of v0, /device:TPU:2, one launch (start us, length us, event | category | flops | bytes accessed | tf_op | source)
XLA Modules:
  0.0 104.8 jit_solution(13523828991145174058)
XLA Ops:
  0.0 2.4 %copy.14 = f32[16,4,2,16,128]{4,3,1,0,2:T(8,128)} copy(f32[16,4,2,16,128]{4,3,2,1,0:T(8,128)} %bitcast.93) | data formatting | bytes 2097152 | tf_op jit(solution)/shard_map/reshape | solution.py:73
  2.4 3.7 %all-to-all-start = ((f32[16,4,2,16,128]{4,3,1,0,2:T(8,128)}), f32[16,4,2,16,128]{4,3,1,0,2:T(8,128)S(1)}, u32[]{:S(2)}, u32[]{:S(2)}) async-start(f32[16,4,2,16,128]{4,3,1,0,2:T(8,128)} %copy.14), calls=%async_computation | async-start | bytes 2097152 | tf_op jit(solution)/shard_map/all_to_all | solution.py:74
  10.1 9.9 %all-to-all-done = f32[16,4,2,16,128]{4,3,1,0,2:T(8,128)S(1)} async-done(((f32[16,4,2,16,128]{4,3,1,0,2:T(8,128)}), f32[16,4,2,16,128]{4,3,1,0,2:T(8,128)S(1)}, u32[]{:S(2)}, u32[]{:S(2)}) %all-to-all-start) | async-done | bytes 1048608 | tf_op jit(solution)/shard_map/all_to_all | solution.py:74
  20.1 5.4 %while.36 = (s32[]{:T(128)}, f32[3,8192]{1,0:T(4,128)S(1)}, f32[8192]{0:T(1024)S(1)}, f32[8192]{0:T(1024)S(1)}, s32[]{:T(128)}, /*index=5*/pred[]{:T(512)}, f32[...) while((s32[]{:T(128)}, f32[3,8192]{1,0:T(4,128)S(1)}, ...), condition=%wide.region_1.2_spmd.clone.clone, body=%wide.region_0.1_spmd.clone.clone.sunk | while | flops 35979272 | bytes 2101500 | solution.py:40
  20.8 0.7 convolution_bitcast_fusion.8
  21.5 0.7 convolution_bitcast_fusion.9
  23.2 0.7 convolution_bitcast_fusion.8
  23.9 0.7 convolution_bitcast_fusion.9
  25.8 39.9 %while.37 = (s32[]{:T(128)}, f32[3,8192]{1,0:T(4,128)S(1)}, f32[8192]{0:T(1024)S(1)}, f32[8192]{0:T(1024)S(1)}, s32[]{:T(128)}, /*index=5*/pred[]{:T(512)}, f32[...) while((s32[]{:T(128)}, f32[3,8192]{1,0:T(4,128)S(1)}, ...), condition=%wide.region_3.4_spmd.clone.clone, body=%wide.region_2.3_spmd.clone.clone.sunk | while | flops 35979272 | bytes 2101500 | solution.py:40
  26.6 0.7 convolution_bitcast_fusion.10
  27.3 0.7 convolution_bitcast_fusion.11
  29.0 0.7 convolution_bitcast_fusion.10
  29.8 0.7 convolution_bitcast_fusion.11
  31.5 0.7 convolution_bitcast_fusion.10
  32.2 0.7 convolution_bitcast_fusion.11
  33.9 0.7 convolution_bitcast_fusion.10
  34.7 0.7 convolution_bitcast_fusion.11
  36.4 0.7 convolution_bitcast_fusion.10
  38.8 0.7 convolution_bitcast_fusion.10
  41.3 0.7 convolution_bitcast_fusion.10
  42.0 0.7 convolution_bitcast_fusion.11
  43.7 0.7 convolution_bitcast_fusion.10
  46.2 0.7 convolution_bitcast_fusion.10
  48.6 0.7 convolution_bitcast_fusion.10
  51.1 0.7 convolution_bitcast_fusion.10
  53.5 0.7 convolution_bitcast_fusion.10
  56.0 0.7 convolution_bitcast_fusion.10
  58.4 0.7 convolution_bitcast_fusion.10
  60.9 0.7 convolution_bitcast_fusion.10
  63.3 0.7 convolution_bitcast_fusion.10
  65.9 0.9 fusion.22
  67.2 36.7 %all_to_all.30 = f32[5,4,16,128]{3,2,0,1:T(8,128)S(1)} all-to-all(f32[5,4,16,128]{3,2,0,1:T(8,128)S(1)} %pad_maximum_fusion.4), channel_id=1, replica_groups=mesh['bx'=4,'by'=4,'bz'=2] {'by'}, dimensions={1} | all-to-all | bytes 327680 | tf_op jit(solution)/shard_map/all_to_all | solution.py:60
  (156 shorter events, 16.2 us)
Async XLA Ops:
  2.4 3.7 %copy-start.3 = (s32[1,4,2]{1,2,0:T(2,128)S(1)}, s32[1,4,2]{1,2,0:T(2,128)}, u32[]{:S(2)}) copy-start(s32[1,4,2]{1,2,0:T(2,128)} %param.13) | copy-start | bytes 100
  2.4 7.0 %copy-start = (f32[3,128]{1,0:T(4,128)S(1)}, f32[3,128]{1,0:T(4,128)}, u32[]{:S(2)}) copy-start(f32[3,128]{1,0:T(4,128)} %param.10) | copy-start | bytes 4612
  2.4 7.0 %copy-start.1 = (f32[128]{0:T(128)S(1)}, f32[128]{0:T(128)}, u32[]{:S(2)}) copy-start(f32[128]{0:T(128)} %param.11) | copy-start | bytes 1540
  2.4 7.1 %copy-start.2 = (s32[1,1,2]{2,1,0:T(1,128)S(1)}, s32[1,1,2]{2,1,0:T(1,128)}, u32[]{:S(2)}) copy-start(s32[1,1,2]{2,1,0:T(1,128)} %param.12) | copy-start | bytes 28
  2.4 17.6 %all-to-all-start = ((f32[16,4,2,16,128]{4,3,1,0,2:T(8,128)}), f32[16,4,2,16,128]{4,3,1,0,2:T(8,128)S(1)}, u32[]{:S(2)}, u32[]{:S(2)}) async-start(f32[16,4,2,16,128]{4,3,1,0,2:T(8,128)} %copy.14), calls=%async_computation | async-start | bytes 2097152 | tf_op jit(solution)/shard_map/all_to_all | solution.py:74
where the time goes:
time: 104 us; the launch traced here: 105 us
  blocking collectives  36.7 us (35%)
  matrix products  27.2 us (26%)
  loops' own time  14.5 us (14%)
  waiting for transfers between devices  9.87 us (9%)
  other arithmetic  5.52 us (5%)
  local copies, waits for them, and re-layouts  5.03 us (5%)
  starting transfers between devices  3.72 us (4%)
  between operations  2.19 us (2%)
    all_to_all x1, blocking collectives, deliver_rows(): return lax.all_to_all(merged, 'by', split_axis=1, concat_axis=3, tiled=True)  36.7 us
    dot_general x36, matrix products, fetch(): joined = jnp.dot(halves, onehot, preferred_element_type=jnp.float32)  26.2 us
    another operation x2, loops' own time, march(): color, depth, trans = lax.fori_loop(0, count, step, start)  14.5 us
    all_to_all x1, waiting for transfers between devices, shards(): column = lax.all_to_all(slab, 'bz', split_axis=2, concat_axis=0, tiled=True)  9.87 us
    all_to_all x1, starting transfers between devices, shards(): column = lax.all_to_all(slab, 'bz', split_axis=2, concat_axis=0, tiled=True)  3.72 us
    reshape x1, local copies, waits for them, and re-layouts, shards(): slab = density.reshape(depth_cells, n_by, n_bz, rows, tile_y)  2.35 us
  transfers between devices with their start and end apart: 1, of which 1 were waited for; matrix products, arithmetic and copies ran while one was open for 2% of the time, Pallas kernels for 0%

commit v1 on v0

v1 whole, which is shorter than its diff:
```python
import functools

import jax
import jax.numpy as jnp
from jax import lax
from jax.experimental import pallas as pl
from jax.experimental.pallas import tpu as pltpu
from jax.sharding import PartitionSpec as P

MESH = pl.DeviceIdType.MESH
LOG2E = 1.4426950408889634


def kernel(
    n_by, n_bz,
    density_ref, colors_ref, extinction_ref, steps_ref, ranks_ref,
    out_ref,
    cells_buf, colors_buf, extinction_buf, parts, got, ready,
    load_sem, table_sem, send_z, recv_z, send_y, recv_y,
):
    me_y, me_z = lax.axis_index("by"), lax.axis_index("bz")
    blocks, depth_cells, rows, lanes = cells_buf.shape
    total = depth_cells * n_bz
    points = colors_buf.shape[1]

    others_z = [lax.rem(me_z + o, n_bz) for o in range(1, n_bz)]
    others_y = [lax.rem(me_y + o, n_by) for o in range(1, n_by)]

    barrier = pltpu.get_barrier_semaphore()
    for k in others_z:
        pl.semaphore_signal(barrier, inc=1, device_id={"bz": k}, device_id_type=MESH)
    for j in others_y:
        pl.semaphore_signal(barrier, inc=1, device_id={"by": j}, device_id_type=MESH)

    def table_loads():
        return (
            pltpu.make_async_copy(colors_ref, colors_buf, table_sem.at[0]),
            pltpu.make_async_copy(extinction_ref, extinction_buf, table_sem.at[1]),
        )

    def load(block):
        return pltpu.make_async_copy(density_ref.at[:, block], cells_buf.at[block], load_sem.at[block])

    def target(step):
        return lax.rem(me_y + 1 + step, n_by)

    for copy in table_loads():
        copy.start()
    for o in range(1, n_bz + 1):
        k = lax.rem(me_z + o, n_bz)

        def start(step, carry, k=k):
            load(target(step) * n_bz + k).start()
            return carry

        lax.fori_loop(0, n_by, start, 0)

    rank = ranks_ref[0, me_y, me_z]
    count = steps_ref[0, 0, me_z]
    backward = ranks_ref[0, 0, 0] != 0
    nearest = (rank * depth_cells).astype(jnp.float32) * (1.0 / total)

    for copy in table_loads():
        copy.wait()
    shape = (rows, lanes)

    def pair(row):
        wide = jnp.broadcast_to(row, (8, points))
        slope = pltpu.roll(wide, points - 1, 1) - wide
        return jnp.broadcast_to(wide[:1], (rows, points)), jnp.broadcast_to(slope[:1], (rows, points))

    tables = [pair(colors_buf[c : c + 1]) for c in range(3)] + [pair(extinction_buf[...])]

    def render(block):
        load(block).wait()
        color = [jnp.zeros(shape, jnp.float32) for _ in range(3)]
        depth = jnp.zeros(shape, jnp.float32)
        trans = jnp.ones(shape, jnp.float32)
        for t in range(depth_cells):
            plane = jnp.where(backward, cells_buf[block, depth_cells - 1 - t], cells_buf[block, t])
            coord = plane * (points - 1)
            index = jnp.minimum(coord.astype(jnp.int32), points - 2)
            frac = coord - index.astype(jnp.float32)

            def lookup(table):
                base, slope = (
                    jnp.take_along_axis(half, index, axis=1, mode="promise_in_bounds") for half in table
                )
                return base + frac * slope

            red, green, blue, kappa = [lookup(table) for table in tables]
            keep = jnp.exp2(kappa * jnp.where(t < count, -LOG2E, 0.0))
            weight = trans * (1.0 - keep)
            color = [c + weight * v for c, v in zip(color, (red, green, blue))]
            depth = depth + weight * (nearest + (t + 0.5) / total)
            trans = trans * keep
        return color + [depth, trans]

    def to_layer(block, step, o):
        k = lax.rem(me_z + o, n_bz)
        return pltpu.make_async_remote_copy(
            src_ref=parts.at[block],
            dst_ref=got.at[me_z, step],
            send_sem=send_z.at[block],
            recv_sem=recv_z.at[me_z, step],
            device_id={"bz": k},
            device_id_type=MESH,
        )

    def from_layer(k, step):
        return pltpu.make_async_remote_copy(
            src_ref=parts.at[0],
            dst_ref=got.at[k, step],
            send_sem=send_z.at[0],
            recv_sem=recv_z.at[k, step],
            device_id={"bz": k},
            device_id_type=MESH,
        )

    def columns(j):
        return pl.ds(pl.multiple_of(j * lanes, lanes), lanes)

    def to_owner(step):
        j = target(step)
        return pltpu.make_async_remote_copy(
            src_ref=ready.at[step],
            dst_ref=out_ref.at[:, :, columns(me_y)],
            send_sem=send_y.at[step],
            recv_sem=recv_y.at[me_y],
            device_id={"by": j},
            device_id_type=MESH,
        )

    def from_column(j):
        return pltpu.make_async_remote_copy(
            src_ref=ready.at[0],
            dst_ref=out_ref.at[:, :, columns(j)],
            send_sem=send_y.at[0],
            recv_sem=recv_y.at[j],
            device_id={"by": j},
            device_id_type=MESH,
        )

    def store(ref, slot, values):
        for c, value in enumerate(values):
            ref[slot, c] = value

    def away(step, carry):
        for o in range(1, n_bz):
            block = target(step) * n_bz + lax.rem(me_z + o, n_bz)
            store(parts, block, render(block))

            if o == 1:

                @pl.when(step == 0)
                def _():
                    pl.semaphore_wait(barrier, n_bz - 1 + n_by - 1)

            to_layer(block, step, o).start()
        return carry

    lax.fori_loop(0, n_by, away, 0)

    def merged(step):
        block = target(step) * n_bz + me_z
        for c, value in enumerate(render(block)):
            got[me_z, step, c] = value
        for o in range(1, n_bz):
            from_layer(lax.rem(me_z + o, n_bz), step).wait_recv()
        total_values = None
        for q in range(n_bz):
            layer = [
                jnp.where(backward, got[n_bz - 1 - q, step, c], got[q, step, c]) for c in range(5)
            ]
            if total_values is None:
                total_values = layer
            else:
                through = total_values[4]
                total_values = [a + through * b for a, b in zip(total_values[:4], layer[:4])]
                total_values.append(through * layer[4])
        return total_values[:4] + [1.0 - total_values[4]]

    def own(step, carry):
        store(ready, step, merged(step))
        to_owner(step).start()
        return carry

    lax.fori_loop(0, n_by - 1, own, 0)
    for c, value in enumerate(merged(n_by - 1)):
        out_ref[c, :, columns(me_y)] = value

    for j in others_y:
        from_column(j).wait_recv()

    def finish(step, carry):
        for o in range(1, n_bz):
            to_layer(target(step) * n_bz + lax.rem(me_z + o, n_bz), step, o).wait_send()
        return carry

    lax.fori_loop(0, n_by, finish, 0)

    def finish_owner(step, carry):
        to_owner(step).wait_send()
        return carry

    lax.fori_loop(0, n_by - 1, finish_owner, 0)


def shards(density, colors, extinction, march_steps, depth_rank):
    n_by = lax.axis_size("by")
    n_bz = lax.axis_size("bz")
    depth_cells, tile_x, tile_y = density.shape
    blocks = n_by * n_bz
    rows = tile_x // blocks
    points = colors.shape[1]
    f32 = jnp.float32
    return pl.pallas_call(
        functools.partial(kernel, n_by, n_bz),
        out_shape=jax.ShapeDtypeStruct((5, rows, n_by * tile_y), f32),
        in_specs=[pl.BlockSpec(memory_space=pl.ANY)] * 3 + [pl.BlockSpec(memory_space=pltpu.SMEM)] * 2,
        out_specs=pl.BlockSpec(memory_space=pltpu.VMEM),
        scratch_shapes=[
            pltpu.VMEM((blocks, depth_cells, rows, tile_y), f32),
            pltpu.VMEM((3, points), f32),
            pltpu.VMEM((1, points), f32),
            pltpu.VMEM((blocks, 5, rows, tile_y), f32),
            pltpu.VMEM((n_bz, n_by, 5, rows, tile_y), f32),
            pltpu.VMEM((n_by, 5, rows, tile_y), f32),
            pltpu.SemaphoreType.DMA((blocks,)),
            pltpu.SemaphoreType.DMA((2,)),
            pltpu.SemaphoreType.DMA((blocks,)),
            pltpu.SemaphoreType.DMA((n_bz, n_by)),
            pltpu.SemaphoreType.DMA((n_by,)),
            pltpu.SemaphoreType.DMA((n_by,)),
        ],
        compiler_params=pltpu.CompilerParams(collective_id=0, has_side_effects=True),
    )(
        density.reshape(depth_cells, blocks, rows, tile_y),
        colors,
        extinction.reshape(1, points),
        march_steps,
        depth_rank,
    )


def solution(mesh):
    return jax.shard_map(
        shards,
        mesh=mesh,
        in_specs=(P("bz", "bx", "by"), P(), P(), P("bx", "by", None), P("bx", None, None)),
        out_specs=P(None, ("bx", "by", "bz"), None),
        check_vma=False,
    )
```

time: 104 us -> 18.2 us (0.17)
  the two profiles are of different devices: /device:TPU:2 before, /device:TPU:0 now
where the time goes in v1:
time: 18.2 us; the launch traced here: 18 us
  Pallas kernels  15 us (82%)
  local copies, waits for them, and re-layouts  2.94 us (16%)
    pallas_call x1, Pallas kernels, shards(): pl.pallas_call(functools.partial(kernel, n_by, n_bz), out_shape=jax.Shape...  15 us
    unnamed x4, local copies, waits for them, and re-layouts  2.94 us

profile of v1, /device:TPU:0, one launch (start us, length us, event | category | flops | bytes accessed | tf_op | source)
XLA Modules:
  0.0 18.0 jit_solution(16158265941335339152)
XLA Ops:
  0.0 0.0 copy-start
  0.0 0.7 %copy-done = s32[1,4,2]{1,2,0:T(2,128)S(1)} copy-done((s32[1,4,2]{1,2,0:T(2,128)S(1)}, s32[1,4,2]{1,2,0:T(2,128)}, u32[]{:S(2)}) %copy-start) | copy-done | bytes 56
  0.7 0.7 %copy.6.ranks_ref = s32[1,4,2]{2,1,0:T(4,128)} copy(s32[1,4,2]{1,2,0:T(2,128)S(1)} %copy-done) | data formatting | bytes 64 | tf_op args[4]
  1.3 15.0 %shard_map.55 = f32[5,16,512]{2,1,0:T(8,128)} custom-call(f32[16,8,16,128]{3,2,1,0:T(8,128)} %bitcast.2, f32[3,128]{1,0:T(4,128)} %colors_ref.1, f32[1,128]{1,0:T(1,128)} %bitcast.3, s32[1,1,2]{2,1,0:T(1,128)} %steps_ref.1, s32[1,4,2]{2,1,0:T(4,128)} %copy.6.ranks_ref), custom_call_target="tpu_custom_call" | custom-call | tf_op jit(solution)/shard_map/pallas_call | solution.py:217
  16.4 1.6 %copy.8 = f32[5,16,512]{2,1,0:T(8,128)} copy(f32[5,16,512]{2,1,0:T(8,128)} %shard_map.55) | data formatting | bytes 327680
Async XLA Ops:
  0.0 0.7 %copy-start = (s32[1,4,2]{1,2,0:T(2,128)S(1)}, s32[1,4,2]{1,2,0:T(2,128)}, u32[]{:S(2)}) copy-start(s32[1,4,2]{1,2,0:T(2,128)} %param.9) | copy-start | bytes 100

commit v2 on v1

--- a/solution.py
+++ b/solution.py
@@ -55,7 +55,7 @@
 
         lax.fori_loop(0, n_by, start, 0)
 
-    rank = ranks_ref[0, me_y, me_z]
+    rank = ranks_ref[0, me_z, me_y]
     count = steps_ref[0, 0, me_z]
     backward = ranks_ref[0, 0, 0] != 0
     nearest = (rank * depth_cells).astype(jnp.float32) * (1.0 / total)
@@ -216,8 +216,8 @@
     f32 = jnp.float32
     return pl.pallas_call(
         functools.partial(kernel, n_by, n_bz),
-        out_shape=jax.ShapeDtypeStruct((5, rows, n_by * tile_y), f32),
-        in_specs=[pl.BlockSpec(memory_space=pl.ANY)] * 3 + [pl.BlockSpec(memory_space=pltpu.SMEM)] * 2,
+        out_shape=pltpu.VMEM((5, rows, n_by * tile_y), f32),
+        in_specs=[pl.BlockSpec(memory_space=pltpu.HBM)] * 3 + [pl.BlockSpec(memory_space=pltpu.SMEM)] * 2,
         out_specs=pl.BlockSpec(memory_space=pltpu.VMEM),
         scratch_shapes=[
             pltpu.VMEM((blocks, depth_cells, rows, tile_y), f32),
@@ -239,7 +239,7 @@
         colors,
         extinction.reshape(1, points),
         march_steps,
-        depth_rank,
+        depth_rank.transpose(0, 2, 1),
     )
 
 

time: 18.2 us -> 15.2 us (0.84)
  local copies, waits for them, and re-layouts: 2.94 us -> 0.67 us
  Pallas kernels: 15 us -> 14.4 us
    unnamed x4 -> x1, local copies, waits for them, and re-layouts: 2.94 us -> 0.67 us
    pallas_call x1, Pallas kernels: 15 us -> 14.4 us  [shards(): pl.pallas_call(functools.partial(kernel, n_by, n_bz), out_shape=pltpu.VME...]
where the time goes in v2:
time: 15.2 us; the launch traced here: 15.1 us
  Pallas kernels  14.4 us (95%)
  local copies, waits for them, and re-layouts  0.67 us (4%)
    pallas_call x1, Pallas kernels, shards(): pl.pallas_call(functools.partial(kernel, n_by, n_bz), out_shape=pltpu.VME...  14.4 us
    unnamed x1, local copies, waits for them, and re-layouts  0.67 us

profile of v2, /device:TPU:0, one launch (start us, length us, event | category | flops | bytes accessed | tf_op | source)
XLA Modules:
  0.0 15.1 jit_solution(4955362818762448418)
XLA Ops:
  0.0 14.4 %shard_map.55 = f32[5,16,512]{2,1,0:T(8,128)S(1)} custom-call(f32[16,8,16,128]{3,2,1,0:T(8,128)} %bitcast.3, f32[3,128]{1,0:T(4,128)} %colors_ref.1, f32[1,128]{1,0:T(1,128)} %bitcast.5, s32[1,1,2]{2,1,0:T(1,128)} %steps_ref.1, s32[1,2,4]{2,1,0:T(2,128)} %bitcast.4), custom_call_target="tpu_custom_call" | custom-call | tf_op jit(solution)/shard_map/pallas_call | solution.py:217
  14.4 0.7 %copy.7 = f32[5,16,512]{2,1,0:T(8,128)} copy(f32[5,16,512]{2,1,0:T(8,128)S(1)} %shard_map.55) | data formatting | bytes 327680

commit v3 on v2

--- a/solution.py
+++ b/solution.py
@@ -9,6 +9,16 @@
 
 MESH = pl.DeviceIdType.MESH
 LOG2E = 1.4426950408889634
+STEPS = 32767
+FINE = 65535
+SHIFT = 65536
+PICK = lax.GatherDimensionNumbers(
+    offset_dims=(),
+    collapsed_slice_dims=(1,),
+    start_index_map=(1,),
+    operand_batching_dims=(0,),
+    start_indices_batching_dims=(0,),
+)
 
 
 def kernel(
@@ -62,39 +72,61 @@
 
     for copy in table_loads():
         copy.wait()
-    shape = (rows, lanes)
-
-    def pair(row):
-        wide = jnp.broadcast_to(row, (8, points))
-        slope = pltpu.roll(wide, points - 1, 1) - wide
-        return jnp.broadcast_to(wide[:1], (rows, points)), jnp.broadcast_to(slope[:1], (rows, points))
-
-    tables = [pair(colors_buf[c : c + 1]) for c in range(3)] + [pair(extinction_buf[...])]
+
+    sub = min(rows, 8)
+
+    def spread(table):
+        return jnp.broadcast_to(table[:1], (sub, points))
+
+    def packed(row):
+        wide = jnp.broadcast_to(jnp.floor(row * STEPS + 0.5), (8, points)).astype(jnp.int32)
+        return spread(wide * SHIFT + (pltpu.roll(wide, points - 1, 1) - wide))
+
+    rgb_tables = [packed(colors_buf[c : c + 1]) for c in range(3)]
+
+    largest = jnp.broadcast_to(jnp.max(extinction_buf[...], axis=1, keepdims=True), (8, points))
+    fine = jnp.floor(extinction_buf[...] * (FINE / largest) + 0.5).astype(jnp.int32)
+    kappa_tables = [spread(fine * SHIFT + pltpu.roll(fine, points - 1, 1))]
+    scale = spread(largest * (-LOG2E / FINE))
+
+    def look_up(block, t, part):
+        at = pl.ds(part * sub, sub)
+        plane = jnp.where(backward, cells_buf[block, depth_cells - 1 - t, at], cells_buf[block, t, at])
+        coord = plane * (points - 1)
+        index = coord.astype(jnp.int32)
+        frac = coord - index.astype(jnp.float32)
+        tilt = frac * SHIFT - 1.0
+
+        def pick(table):
+            return lax.gather(
+                table, index[..., None], PICK, (1, 1), mode=lax.GatherScatterMode.PROMISE_IN_BOUNDS
+            )
+
+        picked = [pick(table) for table in rgb_tables + kappa_tables]
+        rgb = []
+        for both in picked[:3]:
+            step = lax.shift_right_arithmetic(lax.shift_left(both, 16), 16)
+            rgb.append(both.astype(jnp.float32) + step.astype(jnp.float32) * tilt)
+        base = lax.shift_right_logical(picked[3], 16).astype(jnp.float32)
+        kappa = base + frac * ((picked[3] & 65535).astype(jnp.float32) - base)
+        return rgb, kappa
 
     def render(block):
         load(block).wait()
-        color = [jnp.zeros(shape, jnp.float32) for _ in range(3)]
-        depth = jnp.zeros(shape, jnp.float32)
-        trans = jnp.ones(shape, jnp.float32)
+        shape = (sub, lanes)
+        parts_of = []
+        for part in range(rows // sub):
+            parts_of.append([jnp.zeros(shape, jnp.float32)] * 4 + [jnp.ones(shape, jnp.float32)])
         for t in range(depth_cells):
-            plane = jnp.where(backward, cells_buf[block, depth_cells - 1 - t], cells_buf[block, t])
-            coord = plane * (points - 1)
-            index = jnp.minimum(coord.astype(jnp.int32), points - 2)
-            frac = coord - index.astype(jnp.float32)
-
-            def lookup(table):
-                base, slope = (
-                    jnp.take_along_axis(half, index, axis=1, mode="promise_in_bounds") for half in table
-                )
-                return base + frac * slope
-
-            red, green, blue, kappa = [lookup(table) for table in tables]
-            keep = jnp.exp2(kappa * jnp.where(t < count, -LOG2E, 0.0))
-            weight = trans * (1.0 - keep)
-            color = [c + weight * v for c, v in zip(color, (red, green, blue))]
-            depth = depth + weight * (nearest + (t + 0.5) / total)
-            trans = trans * keep
-        return color + [depth, trans]
+            absorb = jnp.where(t < count, scale, 0.0)
+            position = nearest + (t + 0.5) / total
+            for part, (red, green, blue, depth, trans) in enumerate(parts_of):
+                rgb, kappa = look_up(block, t, part)
+                keep = jnp.exp2(kappa * absorb)
+                weight = trans * (1.0 - keep)
+                color = [c + weight * v for c, v in zip((red, green, blue), rgb)]
+                parts_of[part] = color + [depth + weight * position, trans * keep]
+        return [[c * (1.0 / (SHIFT * STEPS)) for c in p[:3]] + p[3:] for p in parts_of]
 
     def to_layer(block, step, o):
         k = lax.rem(me_z + o, n_bz)
@@ -142,13 +174,14 @@
         )
 
     def store(ref, slot, values):
-        for c, value in enumerate(values):
-            ref[slot, c] = value
+        for part, channels in enumerate(values):
+            for c, value in enumerate(channels):
+                ref[(*slot, c, pl.ds(part * sub, sub))] = value
 
     def away(step, carry):
         for o in range(1, n_bz):
             block = target(step) * n_bz + lax.rem(me_z + o, n_bz)
-            store(parts, block, render(block))
+            store(parts, (block,), render(block))
 
             if o == 1:
 
@@ -163,8 +196,7 @@
 
     def merged(step):
         block = target(step) * n_bz + me_z
-        for c, value in enumerate(render(block)):
-            got[me_z, step, c] = value
+        store(got, (me_z, step), render(block))
         for o in range(1, n_bz):
             from_layer(lax.rem(me_z + o, n_bz), step).wait_recv()
         total_values = None
@@ -181,7 +213,9 @@
         return total_values[:4] + [1.0 - total_values[4]]
 
     def own(step, carry):
-        store(ready, step, merged(step))
+        for c, value in enumerate(merged(step)):
+            ready[step, c] = value
+
         to_owner(step).start()
         return carry
 

time: 15.2 us -> 15 us (0.987)
  Pallas kernels: 14.4 us -> 14.1 us
    pallas_call x1, Pallas kernels: 14.4 us -> 14.1 us  [shards(): pl.pallas_call(functools.partial(kernel, n_by, n_bz), out_shape=pltpu.VME...]
where the time goes in v3:
time: 15 us; the launch traced here: 14.8 us
  Pallas kernels  14.1 us (94%)
  local copies, waits for them, and re-layouts  0.67 us (4%)
    pallas_call x1, Pallas kernels, shards(): pl.pallas_call(functools.partial(kernel, n_by, n_bz), out_shape=pltpu.VME...  14.1 us
    unnamed x1, local copies, waits for them, and re-layouts  0.67 us

profile of v3, /device:TPU:0, one launch (start us, length us, event | category | flops | bytes accessed | tf_op | source)
XLA Modules:
  0.0 14.8 jit_solution(3331875589986181744)
XLA Ops:
  0.0 14.1 %shard_map.55 = f32[5,16,512]{2,1,0:T(8,128)S(1)} custom-call(f32[16,8,16,128]{3,2,1,0:T(8,128)} %bitcast.3, f32[3,128]{1,0:T(4,128)} %colors_ref.1, f32[1,128]{1,0:T(1,128)} %bitcast.5, s32[1,1,2]{2,1,0:T(1,128)} %steps_ref.1, s32[1,2,4]{2,1,0:T(2,128)} %bitcast.4), custom_call_target="tpu_custom_call" | custom-call | tf_op jit(solution)/shard_map/pallas_call | solution.py:251
  14.1 0.7 %copy.7 = f32[5,16,512]{2,1,0:T(8,128)} copy(f32[5,16,512]{2,1,0:T(8,128)S(1)} %shard_map.55) | data formatting | bytes 327680

commit v4 on v3

--- a/solution.py
+++ b/solution.py
@@ -23,9 +23,9 @@
 
 def kernel(
     n_by, n_bz,
-    density_ref, colors_ref, extinction_ref, steps_ref, ranks_ref,
+    density_ref, colors_ref, extinction_ref, steps_hbm, ranks_hbm,
     out_ref,
-    cells_buf, colors_buf, extinction_buf, parts, got, ready,
+    cells_buf, colors_buf, extinction_buf, steps_ref, ranks_ref, parts, got, ready,
     load_sem, table_sem, send_z, recv_z, send_y, recv_y,
 ):
     me_y, me_z = lax.axis_index("by"), lax.axis_index("bz")
@@ -46,13 +46,21 @@
         return (
             pltpu.make_async_copy(colors_ref, colors_buf, table_sem.at[0]),
             pltpu.make_async_copy(extinction_ref, extinction_buf, table_sem.at[1]),
+            pltpu.make_async_copy(steps_hbm, steps_ref, table_sem.at[2]),
+            pltpu.make_async_copy(ranks_hbm, ranks_ref, table_sem.at[3]),
         )
 
     def load(block):
         return pltpu.make_async_copy(density_ref.at[:, block], cells_buf.at[block], load_sem.at[block])
 
     def target(step):
-        return lax.rem(me_y + 1 + step, n_by)
+        if n_by & (n_by - 1):
+            return lax.rem(me_y + 1 + step, n_by)
+        flips, column, weight = n_by - 1 - step, 0, 1
+        while weight < n_by:
+            column = column + weight * lax.rem(me_y // weight + flips // weight, 2)
+            weight *= 2
+        return column
 
     for copy in table_loads():
         copy.start()
@@ -65,13 +73,12 @@
 
         lax.fori_loop(0, n_by, start, 0)
 
+    for copy in table_loads():
+        copy.wait()
     rank = ranks_ref[0, me_z, me_y]
     count = steps_ref[0, 0, me_z]
     backward = ranks_ref[0, 0, 0] != 0
     nearest = (rank * depth_cells).astype(jnp.float32) * (1.0 / total)
-
-    for copy in table_loads():
-        copy.wait()
 
     sub = min(rows, 8)
 
@@ -251,17 +258,19 @@
     return pl.pallas_call(
         functools.partial(kernel, n_by, n_bz),
         out_shape=pltpu.VMEM((5, rows, n_by * tile_y), f32),
-        in_specs=[pl.BlockSpec(memory_space=pltpu.HBM)] * 3 + [pl.BlockSpec(memory_space=pltpu.SMEM)] * 2,
+        in_specs=[pl.BlockSpec(memory_space=pl.ANY)] * 5,
         out_specs=pl.BlockSpec(memory_space=pltpu.VMEM),
         scratch_shapes=[
             pltpu.VMEM((blocks, depth_cells, rows, tile_y), f32),
             pltpu.VMEM((3, points), f32),
             pltpu.VMEM((1, points), f32),
+            pltpu.SMEM(march_steps.shape, jnp.int32),
+            pltpu.SMEM((depth_rank.shape[0], depth_rank.shape[2], depth_rank.shape[1]), jnp.int32),
             pltpu.VMEM((blocks, 5, rows, tile_y), f32),
             pltpu.VMEM((n_bz, n_by, 5, rows, tile_y), f32),
             pltpu.VMEM((n_by, 5, rows, tile_y), f32),
             pltpu.SemaphoreType.DMA((blocks,)),
-            pltpu.SemaphoreType.DMA((2,)),
+            pltpu.SemaphoreType.DMA((4,)),
             pltpu.SemaphoreType.DMA((blocks,)),
             pltpu.SemaphoreType.DMA((n_bz, n_by)),
             pltpu.SemaphoreType.DMA((n_by,)),

time: 15 us -> 14.2 us (0.947)
  Pallas kernels: 14.1 us -> 13.4 us
    pallas_call x1, Pallas kernels: 14.1 us -> 13.4 us  [shards(): pl.pallas_call(functools.partial(kernel, n_by, n_bz), out_shape=pltpu.VME...]
where the time goes in v4:
time: 14.2 us; the launch traced here: 14.1 us
  Pallas kernels  13.4 us (94%)
  local copies, waits for them, and re-layouts  0.67 us (5%)
    pallas_call x1, Pallas kernels, shards(): pl.pallas_call(functools.partial(kernel, n_by, n_bz), out_shape=pltpu.VME...  13.4 us
    unnamed x1, local copies, waits for them, and re-layouts  0.67 us

profile of v4, /device:TPU:0, one launch (start us, length us, event | category | flops | bytes accessed | tf_op | source)
XLA Modules:
  0.0 14.1 jit_solution(997469598119902681)
XLA Ops:
  0.0 13.4 %shard_map.55 = f32[5,16,512]{2,1,0:T(8,128)S(1)} custom-call(f32[16,8,16,128]{3,2,1,0:T(8,128)} %bitcast.3, f32[3,128]{1,0:T(4,128)} %colors_ref.1, f32[1,128]{1,0:T(1,128)} %bitcast.5, s32[1,1,2]{2,1,0:T(1,128)} %steps_hbm.1, s32[1,2,4]{2,1,0:T(2,128)} %bitcast.4), custom_call_target="tpu_custom_call" | custom-call | tf_op jit(solution)/shard_map/pallas_call | solution.py:258
  13.4 0.7 %copy.7 = f32[5,16,512]{2,1,0:T(8,128)} copy(f32[5,16,512]{2,1,0:T(8,128)S(1)} %shard_map.55) | data formatting | bytes 327680

commit v5 on v4

--- a/solution.py
+++ b/solution.py
@@ -30,6 +30,7 @@
 ):
     me_y, me_z = lax.axis_index("by"), lax.axis_index("bz")
     blocks, depth_cells, rows, lanes = cells_buf.shape
+    pieces = out_ref.shape[1] // rows
     total = depth_cells * n_bz
     points = colors_buf.shape[1]
 
@@ -55,23 +56,26 @@
 
     def target(step):
         if n_by & (n_by - 1):
-            return lax.rem(me_y + 1 + step, n_by)
-        flips, column, weight = n_by - 1 - step, 0, 1
+            return lax.rem(me_y + 1 + step // pieces, n_by)
+        flips, column, weight = n_by - 1 - step // pieces, 0, 1
         while weight < n_by:
             column = column + weight * lax.rem(me_y // weight + flips // weight, 2)
             weight *= 2
         return column
 
+    def block_of(step, k):
+        return (target(step) * n_bz + k) * pieces + lax.rem(step, pieces)
+
     for copy in table_loads():
         copy.start()
     for o in range(1, n_bz + 1):
         k = lax.rem(me_z + o, n_bz)
 
         def start(step, carry, k=k):
-            load(target(step) * n_bz + k).start()
+            load(block_of(step, k)).start()
             return carry
 
-        lax.fori_loop(0, n_by, start, 0)
+        lax.fori_loop(0, n_by * pieces, start, 0)
 
     for copy in table_loads():
         copy.wait()
@@ -156,26 +160,30 @@
             device_id_type=MESH,
         )
 
+    def place(j, piece):
+        at = pl.multiple_of(piece * rows, rows)
+        return out_ref.at[:, pl.ds(at, rows), columns(j)]
+
     def columns(j):
         return pl.ds(pl.multiple_of(j * lanes, lanes), lanes)
 
     def to_owner(step):
-        j = target(step)
+        piece = lax.rem(step, pieces)
         return pltpu.make_async_remote_copy(
             src_ref=ready.at[step],
-            dst_ref=out_ref.at[:, :, columns(me_y)],
+            dst_ref=place(me_y, piece),
             send_sem=send_y.at[step],
-            recv_sem=recv_y.at[me_y],
-            device_id={"by": j},
+            recv_sem=recv_y.at[me_y * pieces + piece],
+            device_id={"by": target(step)},
             device_id_type=MESH,
         )
 
-    def from_column(j):
+    def from_column(j, piece):
         return pltpu.make_async_remote_copy(
             src_ref=ready.at[0],
-            dst_ref=out_ref.at[:, :, columns(j)],
+            dst_ref=place(j, piece),
             send_sem=send_y.at[0],
-            recv_sem=recv_y.at[j],
+            recv_sem=recv_y.at[j * pieces + piece],
             device_id={"by": j},
             device_id_type=MESH,
         )
@@ -187,7 +195,7 @@
 
     def away(step, carry):
         for o in range(1, n_bz):
-            block = target(step) * n_bz + lax.rem(me_z + o, n_bz)
+            block = block_of(step, lax.rem(me_z + o, n_bz))
             store(parts, (block,), render(block))
 
             if o == 1:
@@ -199,10 +207,10 @@
             to_layer(block, step, o).start()
         return carry
 
-    lax.fori_loop(0, n_by, away, 0)
+    lax.fori_loop(0, n_by * pieces, away, 0)
 
     def merged(step):
-        block = target(step) * n_bz + me_z
+        block = block_of(step, me_z)
         store(got, (me_z, step), render(block))
         for o in range(1, n_bz):
             from_layer(lax.rem(me_z + o, n_bz), step).wait_recv()
@@ -226,38 +234,42 @@
         to_owner(step).start()
         return carry
 
-    lax.fori_loop(0, n_by - 1, own, 0)
-    for c, value in enumerate(merged(n_by - 1)):
-        out_ref[c, :, columns(me_y)] = value
+    lax.fori_loop(0, (n_by - 1) * pieces, own, 0)
+    for piece in range(pieces):
+        for c, value in enumerate(merged((n_by - 1) * pieces + piece)):
+            out_ref[c, pl.ds(piece * rows, rows), columns(me_y)] = value
 
     for j in others_y:
-        from_column(j).wait_recv()
+        for piece in range(pieces):
+            from_column(j, piece).wait_recv()
 
     def finish(step, carry):
         for o in range(1, n_bz):
-            to_layer(target(step) * n_bz + lax.rem(me_z + o, n_bz), step, o).wait_send()
+            to_layer(block_of(step, lax.rem(me_z + o, n_bz)), step, o).wait_send()
         return carry
 
-    lax.fori_loop(0, n_by, finish, 0)
+    lax.fori_loop(0, n_by * pieces, finish, 0)
 
     def finish_owner(step, carry):
         to_owner(step).wait_send()
         return carry
 
-    lax.fori_loop(0, n_by - 1, finish_owner, 0)
+    lax.fori_loop(0, (n_by - 1) * pieces, finish_owner, 0)
 
 
 def shards(density, colors, extinction, march_steps, depth_rank):
     n_by = lax.axis_size("by")
     n_bz = lax.axis_size("bz")
     depth_cells, tile_x, tile_y = density.shape
-    blocks = n_by * n_bz
-    rows = tile_x // blocks
+    owned = tile_x // (n_by * n_bz)
+    rows = owned if owned % 8 else 8
+    steps = n_by * (owned // rows)
+    blocks = n_bz * steps
     points = colors.shape[1]
     f32 = jnp.float32
     return pl.pallas_call(
         functools.partial(kernel, n_by, n_bz),
-        out_shape=pltpu.VMEM((5, rows, n_by * tile_y), f32),
+        out_shape=pltpu.VMEM((5, owned, n_by * tile_y), f32),
         in_specs=[pl.BlockSpec(memory_space=pl.ANY)] * 5,
         out_specs=pl.BlockSpec(memory_space=pltpu.VMEM),
         scratch_shapes=[
@@ -267,14 +279,14 @@
             pltpu.SMEM(march_steps.shape, jnp.int32),
             pltpu.SMEM((depth_rank.shape[0], depth_rank.shape[2], depth_rank.shape[1]), jnp.int32),
             pltpu.VMEM((blocks, 5, rows, tile_y), f32),
-            pltpu.VMEM((n_bz, n_by, 5, rows, tile_y), f32),
-            pltpu.VMEM((n_by, 5, rows, tile_y), f32),
+            pltpu.VMEM((n_bz, steps, 5, rows, tile_y), f32),
+            pltpu.VMEM((steps, 5, rows, tile_y), f32),
             pltpu.SemaphoreType.DMA((blocks,)),
             pltpu.SemaphoreType.DMA((4,)),
             pltpu.SemaphoreType.DMA((blocks,)),
-            pltpu.SemaphoreType.DMA((n_bz, n_by)),
-            pltpu.SemaphoreType.DMA((n_by,)),
-            pltpu.SemaphoreType.DMA((n_by,)),
+            pltpu.SemaphoreType.DMA((n_bz, steps)),
+            pltpu.SemaphoreType.DMA((steps,)),
+            pltpu.SemaphoreType.DMA((steps,)),
         ],
         compiler_params=pltpu.CompilerParams(collective_id=0, has_side_effects=True),
     )(

time: 14.2 us -> 14.3 us (level)
  no operation moved by 1% of the time
where the time goes in v5:
time: 14.3 us; the launch traced here: 14.2 us
  Pallas kernels  13.5 us (94%)
  local copies, waits for them, and re-layouts  0.67 us (5%)
    pallas_call x1, Pallas kernels, shards(): pl.pallas_call(functools.partial(kernel, n_by, n_bz), out_shape=pltpu.VME...  13.5 us
    unnamed x1, local copies, waits for them, and re-layouts  0.67 us

profile of v5, /device:TPU:0, one launch (start us, length us, event | category | flops | bytes accessed | tf_op | source)
XLA Modules:
  0.0 14.2 jit_solution(820133920546611492)
XLA Ops:
  0.0 13.5 %shard_map.55 = f32[5,16,512]{2,1,0:T(8,128)S(1)} custom-call(f32[16,16,8,128]{3,2,1,0:T(8,128)} %bitcast.3, f32[3,128]{1,0:T(4,128)} %colors_ref.1, f32[1,128]{1,0:T(1,128)} %bitcast.5, s32[1,1,2]{2,1,0:T(1,128)} %steps_hbm.1, s32[1,2,4]{2,1,0:T(2,128)} %bitcast.4), custom_call_target="tpu_custom_call" | custom-call | tf_op jit(solution)/shard_map/pallas_call | solution.py:270
  13.5 0.7 %copy.7 = f32[5,16,512]{2,1,0:T(8,128)} copy(f32[5,16,512]{2,1,0:T(8,128)S(1)} %shard_map.55) | data formatting | bytes 327680
